TPU v7x, 768 devices: a whole 4x8x12 slice. The times are simulated.
768 devices in a mesh: seq: 12 (over z_lo, x), exp: 64 (over z_hi, y, core).
Axes of the slice: x: 4, y: 8, z: 12 (z_hi: 4, z_lo: 3; z = z_hi * 3 + z_lo), core: 2. Of those that a mesh axis runs over, the one named last changes fastest.
Arguments:
- query: bfloat16 [1536, 8192], P('seq', 'exp'), may hold values from -6 to 6
- key_in: bfloat16 [1536, 8192], P('seq', 'exp'), may hold values from -6 to 6
- value: bfloat16 [1536, 8192], P('seq', 'exp'), may hold values from -6 to 6
- decay_log: float32 [1536, 64], P('seq', 'exp'), may hold values from -1 to 0
- norm_gain: bfloat16 [8192], P('exp'), may hold values from 0.099609375 to 1.8984375
- w_out: bfloat16 [8192, 4096], P('exp'), may hold values from -0.0625 to 0.0625
- router: bfloat16 [4096, 4], replicated, may hold values from -0.09375 to 0.09375
- routes: int32 [1536, 2], P('seq'), may hold values from 0 to 3, all different within a row; in each aligned block of 128 rows (0 to 127, 128 to 255, ...) at most 96 rows name the same one
- w_gate: bfloat16 [64, 4096, 288], P('exp'), may hold values from -0.09375 to 0.09375
- w_up: bfloat16 [64, 4096, 288], P('exp'), may hold values from -0.09375 to 0.09375
- w_down: bfloat16 [64, 288, 4096], P('exp'), may hold values from -0.09375 to 0.09375
Outputs:
- output: bfloat16 [1536, 4096], P(('seq', 'exp'))
Inputs may be any that keep to these rules, and one draw needn't show every extreme that they name: `routes`: among the positions of one block of 128 positions no expert is named more than 96 times, a bound that some block reaches; a position names 2 different experts.
All inputs are finite; a program needn't handle non-finite values.
Results may differ from a plain program's by a relative error of at most 0.015.
Values may be sent and summed in bfloat16 or wider, within the bound.
A program may use at most 32 MiB of HBM per device.

v0:
```python
import jax
import jax.numpy as jnp
from jax import lax
from jax.sharding import PartitionSpec as P


def carried_in(array, axis, combine, identity):
    length, index = (lax.axis_size(axis), lax.axis_index(axis))
    everything = jax.tree.map(
        lambda part, kind: lax.all_gather(part.astype(kind), axis),
        array,
        (jnp.bfloat16, jnp.bfloat16),
    )
    start = jax.tree.map(
        lambda part, zero: jnp.broadcast_to(jnp.asarray(zero, part.dtype), part.shape),
        array,
        identity,
    )

    def turn(k, before):
        reached = k < index
        new = combine(
            before, jax.tree.map(lambda part, own: part[k].astype(own.dtype), everything, array)
        )
        return jax.tree.map(lambda a, b: jnp.where(reached, a, b), new, before)

    return lax.fori_loop(0, length, turn, start)


def chain_combine(earlier, later):
    return (earlier[0] * later[0], later[0][:, None, None] * earlier[1] + later[1])


def local(query, key_in, value, decay_log, norm_gain, w_out, router, routes, w_gate, w_up, w_down):
    tok_count = query.shape[0]
    head_count = decay_log.shape[1]
    head_size = query.shape[1] // head_count
    top_count = routes.shape[1]
    expert_count = router.shape[1]
    capacity = max(2, 3 * tok_count * top_count // (2 * expert_count))
    exp_count = lax.axis_size("exp")
    slice_count = exp_count // expert_count
    queries = query.reshape(tok_count, head_count, head_size)
    keys_local = key_in.reshape(tok_count, head_count, head_size)
    values_local = value.reshape(tok_count, head_count, head_size)
    cumulative = jnp.cumsum(decay_log, axis=0)
    scores = jnp.einsum("thd,shd->hts", queries, keys_local, preferred_element_type=jnp.float32)
    spread = cumulative.T[:, :, None] - cumulative.T[:, None, :]
    causal = jnp.arange(tok_count)[:, None] >= jnp.arange(tok_count)[None, :]
    weights = jnp.where(causal, jnp.exp(jnp.where(causal, spread, 0.0)), 0.0)
    attend = (scores * weights / head_size).astype(jnp.bfloat16)
    intra_part = jnp.einsum(
        "hts,she->the", attend, values_local, preferred_element_type=jnp.float32
    )
    totals = cumulative[-1]
    tail_decay = jnp.exp(totals[None, :] - cumulative)
    state_delta = jnp.einsum(
        "shd,she->hde",
        keys_local.astype(jnp.float32) * tail_decay[:, :, None],
        values_local.astype(jnp.float32),
        precision=lax.Precision.HIGHEST,
    )
    decay_total = jnp.exp(totals)
    _, incoming = carried_in(
        (decay_total, state_delta),
        "seq",
        chain_combine,
        (jnp.ones_like(decay_total), jnp.zeros_like(state_delta)),
    )
    inter_part = (
        jnp.exp(cumulative)[:, :, None]
        * jnp.einsum(
            "thd,hde->the", queries.astype(jnp.float32), incoming, precision=lax.Precision.HIGHEST
        )
        / head_size
    )
    attended = intra_part + inter_part
    inverse_rms = lax.rsqrt(jnp.mean(attended * attended, axis=-1, keepdims=True) + 1e-06)
    gain_f32 = norm_gain.astype(jnp.float32).reshape(head_count, head_size)
    normed = (
        (attended * inverse_rms * gain_f32)
        .astype(jnp.bfloat16)
        .reshape(tok_count, head_count * head_size)
    )
    own_mixed = lax.psum_scatter(
        jnp.dot(normed, w_out, preferred_element_type=jnp.float32),
        "exp",
        scatter_dimension=0,
        tiled=True,
    ).astype(jnp.bfloat16)
    mixed = lax.all_gather(own_mixed, "exp", axis=0, tiled=True)
    logits = jnp.dot(mixed, router, preferred_element_type=jnp.float32)
    member = routes[:, :, None] == jnp.arange(expert_count)[None, None, :]
    picked = jnp.sum(jnp.where(member, logits[:, None, :], 0.0), axis=-1)
    raised = jnp.exp(picked)
    gate_probs = raised / jnp.sum(raised, axis=-1, keepdims=True)
    my_expert = lax.axis_index("exp") // slice_count
    flat_hit = (routes.reshape(-1) == my_expert).astype(jnp.int32)
    slot_flat = jnp.cumsum(flat_hit) - flat_hit
    slot_match = (slot_flat[:, None] == jnp.arange(capacity)[None, :]) & (flat_hit[:, None] > 0)
    token_select = jnp.sum(
        slot_match.reshape(tok_count, top_count, capacity).astype(jnp.float32), axis=1
    )
    token_gate = jnp.sum(jnp.where(routes == my_expert, gate_probs, 0.0), axis=1)
    slot_rows = jnp.dot(
        token_select.astype(jnp.bfloat16).T, mixed, preferred_element_type=jnp.float32
    ).astype(jnp.bfloat16)
    gate_part = jnp.dot(slot_rows, w_gate[0], preferred_element_type=jnp.float32)
    up_part = jnp.dot(slot_rows, w_up[0], preferred_element_type=jnp.float32)
    hidden = (jax.nn.silu(gate_part) * up_part).astype(jnp.bfloat16)
    slice_out = jnp.dot(hidden, w_down[0], preferred_element_type=jnp.float32)
    spread_out = jnp.dot(token_select, slice_out, precision=lax.Precision.HIGHEST)
    summed = lax.psum_scatter(
        token_gate[:, None] * spread_out, "exp", scatter_dimension=0, tiled=True
    )
    return (own_mixed.astype(jnp.float32) + summed).astype(jnp.bfloat16)


def solution(mesh):
    placed = (
        P("seq", "exp"),
        P("seq", "exp"),
        P("seq", "exp"),
        P("seq", "exp"),
        P("exp"),
        P("exp", None),
        P(),
        P("seq", None),
        P("exp", None, None),
        P("exp", None, None),
        P("exp", None, None),
    )
    return jax.shard_map(
        local, mesh=mesh, in_specs=placed, out_specs=P(("seq", "exp"), None), check_vma=False
    )
```

profile of v0, /device:TPU:1, one launch (start us, length us, event | category | flops | bytes accessed | tf_op | source)
XLA Modules:
  0.0 1174.5 jit_solution(3454820613632566514)
XLA Ops:
  6.5 0.8 convert_element_type.89
  7.4 1.4 copy.39
  8.8 1.0 reduce_window_sum.27
  9.8 0.6 slice.13
  11.1 1.3 dynamic-slice
  12.5 0.7 dynamic-update-slice
  13.2 0.1 reduce.2
  13.3 28.0 %all-reduce = bf16[12]{0:T(256)(128)(2,1)S(1)} all-reduce(bf16[12]{0:T(256)(128)(2,1)S(1)} %dynamic-update-slice), channel_id=1, replica_groups=mesh['seq'=12,'exp'=64] {'seq'}, use_global_device_ids=true, to_apply=%add | all-reduce | flops 12 | bytes 48
  41.3 0.7 fusion.51
  42.0 1.1 convolution_convert_fusion.1
  43.1 23.6 %all-gather = bf16[1536,128]{1,0:T(8,128)(2,1)} all-gather(bf16[128,128]{1,0:T(8,128)(2,1)S(1)} %convolution_convert_fusion.1), channel_id=2, replica_groups=mesh['seq'=12,'exp'=64] {'seq'}, dimensions={0}, use_global_device_ids=true | all-gather | bytes 425984 | tf_op jit(solution)/shard_map/all_gather | solution.py:10
  66.7 24.5 %while.14 = (s32[]{:T(128)}, f32[1,128,128]{2,1,0:T(8,128)S(1)}, s32[]{:T(128)}, bf16[12,1]{0,1:T(2,128)(2,1)S(1)}, bf16[12,1,128,128]{3,2,1,0:T(8,128)(2,1)}, /*index=5*/s32[]{:T(128)}, s32[]{:T(128)}) while((s32[]{:T(128)}, f32[1,128,128]{2,1,0:T(8,128)S(1)}, s32[]{:T(128)}, bf16[12,1]{0,1:T(2,128)(2,1)S(1)}, ...), condition=%wide.region_2.3_spmd.clone, body=%wide.region_1.2_spmd.clone.sunk | while | flops 81925 | bytes 163967 | solution.py:27
  66.7 0.6 constant_dynamic-slice_fusion.2
  67.9 0.8 fusion.67
  68.7 0.6 constant_dynamic-slice_fusion.2
  70.0 0.8 fusion.67
  70.8 0.6 constant_dynamic-slice_fusion.2
  72.0 0.8 fusion.67
  72.8 0.6 constant_dynamic-slice_fusion.2
  74.1 0.8 fusion.67
  74.9 0.6 constant_dynamic-slice_fusion.2
  76.1 0.8 fusion.67
  76.9 0.6 constant_dynamic-slice_fusion.2
  78.2 0.8 fusion.67
  79.0 0.6 constant_dynamic-slice_fusion.2
  80.2 0.8 fusion.67
  81.0 0.6 constant_dynamic-slice_fusion.2
  82.2 0.8 fusion.67
  83.1 0.6 constant_dynamic-slice_fusion.2
  84.3 0.8 fusion.67
  85.1 0.6 constant_dynamic-slice_fusion.2
  86.3 0.8 fusion.67
  87.1 0.6 constant_dynamic-slice_fusion.2
  88.4 0.8 fusion.67
  89.2 0.6 constant_dynamic-slice_fusion.2
  90.4 0.8 fusion.67
  91.2 1.0 fusion.18
  92.2 1.1 multiply_reduce_fusion
  93.4 1.9 fusion.35
  95.3 338.5 %all-reduce.7 = bf16[128,4096]{1,0:T(8,128)(2,1)S(1)} all-reduce(f32[128,4096]{1,0:T(8,128)} %fusion.35), channel_id=3, replica_groups=mesh['seq'=12,'exp'=64] {'exp'}, use_global_device_ids=true, to_apply=%region_4.5.clone | all-reduce | flops 524288 | bytes 3145728
  433.8 1.3 dynamic-slice.1
  435.8 0.6 fusion.47
  436.4 0.0 all-gather.4.cloned.1.call-update
  436.4 0.0 all-reduce.6.cloned.1.call-start
  436.5 94.7 %all-gather.4.cloned.1.call-done = bf16[64,2,4096]{2,1,0:T(2,128)(2,1)} async-done(((bf16[1,2,4096]{2,1,0:T(2,128)(2,1)}), bf16[64,2,4096]{2,1,0:T(2,128)(2,1)}) %all-gather.4.cloned.1.call-update) | async-done | bytes 1048592 | tf_op jit(solution)/shard_map/all_gather | solution.py:91
  531.2 1.5 reshape.182
  532.7 0.4 fusion.52
  533.2 0.1 copy.41
  533.3 0.1 reshape.176
  533.4 0.3 reduce-window.9
  533.7 0.1 slice.11
  533.8 0.1 reshape.171
  534.0 0.1 slice_reduce_fusion
  534.1 0.1 broadcast.75
  534.2 0.1 reshape.173
  534.3 0.1 copy.42
  534.4 0.4 convolution_convert_fusion
  534.8 0.9 copy-done.1
  535.6 2.6 fusion.5
  538.3 5.3 fusion.1
  543.6 4.5 convolution_multiply_fusion
  548.1 0.0 all-reduce.6.cloned.1.call-update
  548.1 617.9 %all-reduce.6.cloned.1.call-done = f32[128,4096]{1,0:T(8,128)} async-done(((f32[128,4096]{1,0:T(8,128)}), f32[128,4096]{1,0:T(8,128)}) %all-reduce.6.cloned.1.call-update) | async-done | bytes 2097168
  1166.1 1.5 fusion.37
  (22 shorter events, 0.2 us)
Async XLA Ops:
  6.5 531.7 %copy-start = (bf16[1,288,4096]{2,1,0:T(8,128)(2,1)S(1)}, bf16[1,288,4096]{2,1,0:T(8,128)(2,1)}, u32[]{:S(2)}) copy-start(bf16[1,288,4096]{2,1,0:T(8,128)(2,1)} %param.23) | copy-start | bytes 7077892
  6.5 86.8 %copy-start.3 = (bf16[128,4096]{1,0:T(8,128)(2,1)S(1)}, bf16[128,4096]{1,0:T(8,128)(2,1)}, u32[]{:S(2)}) copy-start(bf16[128,4096]{1,0:T(8,128)(2,1)} %param.18) | copy-start | bytes 3145732
  6.5 524.7 %all-gather.4.cloned.1.call-start = ((), (), s32[]{:S(2)}) async-start(), calls=%async_computation | async-start | bytes 1064960 | tf_op jit(solution)/shard_map/all_gather | solution.py:91
  95.3 437.4 %copy-start.4 = (bf16[4096,4]{0,1:T(4,128)(2,1)S(1)}, bf16[4096,4]{0,1:T(4,128)(2,1)}, u32[]{:S(2)}) copy-start(bf16[4096,4]{0,1:T(4,128)(2,1)} %param.19) | copy-start | bytes 98308
  433.8 2.7 copy-start.2
  433.8 99.3 %copy-start.5 = (s32[128,2]{0,1:T(2,128)S(1)}, s32[128,2]{0,1:T(2,128)}, u32[]{:S(2)}) copy-start(s32[128,2]{0,1:T(2,128)} %param.20) | copy-start | bytes 3076
  436.4 729.6 %all-reduce.6.cloned.1.call-start = ((), (), s32[]{:S(2)}) async-start(), calls=%async_computation.1 | async-start | bytes 4194304
  534.7 0.9 copy-start.1
Sparse Core Ops, SparseCore 0:
  436.5 94.6 all-gather.3
  548.3 617.7 all-reduce.5
where the time goes:
time: 1180 us; the launch traced here: 1170 us
  waiting for transfers between devices  713 us (60%)
  blocking collectives  390 us (33%)
  matrix products  18.3 us (2%)
  local copies, waits for them, and re-layouts  16.4 us (1%)
  between operations  15 us (1%)
  other arithmetic  14.2 us (1%)
    unnamed x3, waiting for transfers between devices  618 us
    unnamed x2, blocking collectives  366 us
    all_gather x1, waiting for transfers between devices, local(): mixed = lax.all_gather(own_mixed, 'exp', axis=0, tiled=True)  94.7 us
    all_gather x1, blocking collectives, carried_in(): lax.all_gather(part.astype(kind), axis)  23.6 us
  transfers between devices with their start and end apart: 2, of which 2 were waited for; matrix products, arithmetic and copies ran while one was open for 0% of the time, Pallas kernels for 0%

commit v1 on v0

v1 whole, which is shorter than its diff:
```python
import jax
import jax.numpy as jnp
from jax import lax
from jax.experimental import pallas as pl
from jax.experimental.pallas import tpu as pltpu
from jax.sharding import PartitionSpec as P

MESH = pl.DeviceIdType.MESH
F32, BF16 = jnp.float32, jnp.bfloat16

NX, NZL, NY, NZH = 4, 3, 8, 4
TOK, HEAD, DM, FFW, EXPERTS = 128, 128, 4096, 288, 4
HALF = DM // 2
CH = TOK // NY
GR = CH // NZH
FPAD = 384
NP = 4
W = HALF // NP
PACK = TOK + 16


def hops_of(piece):
    return (4, 3) if piece % 2 == 0 else (3, 4)


def cols_of(piece):
    return slice(piece * W, (piece + 1) * W)


def dot(a, b):
    return jnp.dot(a, b, preferred_element_type=F32)


def dot_nt(a, b):
    return lax.dot_general(a, b, (((1,), (1,)), ((), ())), preferred_element_type=F32)


def dot_tn(a, b):
    return lax.dot_general(a, b, (((0,), (0,)), ((), ())), preferred_element_type=F32)


def log_rows(total):
    high = total.astype(BF16)
    rest = total - high.astype(F32)
    mid = rest.astype(BF16)
    low = (rest - mid.astype(F32)).astype(BF16)
    row = lax.broadcasted_iota(jnp.int32, (16, HEAD), 0)
    return jnp.where(
        row == 0, high.astype(F32), jnp.where(row == 1, mid.astype(F32), low.astype(F32))
    ).astype(BF16)


def log_of(rows):
    rows = rows.astype(F32)
    return rows[0:1] + rows[1:2] + rows[2:3]


def kernel(
    q_hbm, k_hbm, v_hbm, dec_hbm, gain_hbm, wo_hbm, rt_hbm, routes_hbm, wg_hbm, wu_hbm, wd_hbm,
    out_ref,
    q_v, k_v, v_v, dec_v, gain_v, wo2, rt_v, routes_v, wg_v, wu_v, wd2,
    st_s, st_r, rw_s, rw_r, s_in, nb, part, s1, r1, acc_v, z_s, z_r, mx, hb, s2, r2,
    zh_acc, zh_s, zh_r, fin_s, fin_r,
    ld, st_ss, st_rs, rw_ss, rw_rs, pr_ss, pr_rs, s1_ss, s1_rs, z_ss, z_rs, ag_ss, ag_rs, pf_ss, pf_rs,
    s2_ss, s2_rs, zh_ss, zh_rs,
):
    seq = lax.axis_index("seq")
    ex = lax.axis_index("exp")
    zl, x = seq // NX, seq % NX
    c = ex % 2
    y = (ex // 2) % NY
    zh = ex // (2 * NY)

    def exp_id(zh_, y_, c_):
        return (zh_ * NY + y_) * 2 + c_

    partner = (seq, exp_id(zh, y, 1 - c))
    up = (seq, exp_id(zh, (y + 1) % NY, c))
    down = (seq, exp_id(zh, (y + NY - 1) % NY, c))
    ynb = (up, down)
    za_i, zb_i = zh + 1 - 2 * (zh % 2), NZH - 1 - zh
    za, zb = (seq, exp_id(za_i, y, c)), (seq, exp_id(zb_i, y, c))
    row_peers = [(zl * NX + (x + d) % NX, ex) for d in (1, 2, 3)]
    col_peers = [(((zl + d) % NZL) * NX + x, ex) for d in (1, 2)]

    barrier = pltpu.get_barrier_semaphore()
    peers = [partner, up, down, za, zb] + row_peers + col_peers
    for peer in peers:
        pl.semaphore_signal(barrier, inc=1, device_id=peer, device_id_type=MESH)

    half = pl.multiple_of(c * HALF, HALF)
    other = pl.multiple_of((1 - c) * HALF, HALF)
    loads = [
        pltpu.make_async_copy(src, dst, ld.at[i])
        for i, (src, dst) in enumerate(
            [
                (k_hbm, k_v),
                (v_hbm, v_v),
                (dec_hbm, dec_v),
                (q_hbm, q_v),
                (gain_hbm, gain_v),
                (routes_hbm, routes_v),
                (wo_hbm.at[:, pl.ds(half, HALF)], wo2.at[0:HEAD]),
                (rt_hbm, rt_v),
                (wg_hbm, wg_v),
                (wu_hbm, wu_v),
                (wd_hbm.at[:, pl.ds(half, HALF)], wd2.at[0:FFW]),
            ]
        )
    ]
    for load in loads:
        load.start()

    def remote(src, dst, send, recv, device):
        return pltpu.make_async_remote_copy(
            src_ref=src, dst_ref=dst, send_sem=send, recv_sem=recv,
            device_id=device, device_id_type=MESH,
        )

    sent = []

    def push(*args):
        copy = remote(*args)
        copy.start()
        sent.append(copy)
        return copy

    row_i = lax.broadcasted_iota(jnp.int32, (TOK, TOK), 0)
    col_i = lax.broadcasted_iota(jnp.int32, (TOK, TOK), 1)
    tok_i = (row_i % CH) // GR * (NY * GR) + row_i // CH * GR + row_i % GR

    loads[2].wait()
    dec_row = dec_v[...]
    dec_full = jnp.broadcast_to(dec_row, (TOK, TOK))
    dec_col = jnp.sum(jnp.where(row_i == col_i, dec_full, 0.0), axis=1, keepdims=True)
    cum_row = jnp.sum(jnp.where(row_i <= col_i, dec_col, 0.0), axis=0, keepdims=True)
    cum_col = jnp.sum(jnp.where(col_i <= row_i, dec_full, 0.0), axis=1, keepdims=True)
    cum_tok = jnp.sum(jnp.where(col_i <= tok_i, dec_full, 0.0), axis=1, keepdims=True)
    total = jnp.broadcast_to(jnp.sum(dec_row, axis=1, keepdims=True), (1, HEAD))
    loads[0].wait()
    loads[1].wait()
    tail = jnp.exp(total[:, 0:1] - cum_col)
    keys = k_v[...]
    values = v_v[...]
    delta = dot_tn((keys.astype(F32) * tail).astype(BF16), values)
    st_s[0:TOK, :] = delta.astype(BF16)
    st_s[TOK:PACK, :] = log_rows(total)

    pl.semaphore_wait(barrier, len(peers))
    for d in (1, 2, 3):
        push(st_s, st_r.at[d - 1], st_ss.at[d - 1], st_rs.at[d - 1], row_peers[d - 1])
    wo_copy = push(
        wo_hbm.at[:, pl.ds(other, HALF)], wo2.at[HEAD : 2 * HEAD], pr_ss.at[0], pr_rs.at[0], partner
    )
    wd_copy = push(
        wd_hbm.at[:, pl.ds(other, HALF)], wd2.at[FPAD : FPAD + FFW], pr_ss.at[1], pr_rs.at[1], partner
    )
    wd2[FFW:FPAD, :] = jnp.zeros((FPAD - FFW, HALF), BF16)
    wd2[FPAD + FFW : 2 * FPAD, :] = jnp.zeros((FPAD - FFW, HALF), BF16)

    loads[3].wait()
    to_rows = jnp.where(col_i == tok_i, 1.0, 0.0).astype(BF16)
    queries = dot(to_rows, q_v[...]).astype(BF16)
    causal = col_i <= tok_i
    scores = dot_nt(queries, keys)
    weights = jnp.where(causal, jnp.exp(jnp.where(causal, cum_tok - cum_row, 0.0)), 0.0)
    intra = dot((scores * weights / HEAD).astype(BF16), values)

    loads[5].wait()
    routes = routes_v[...].astype(F32)
    wanted = [
        jnp.sum(
            jnp.where(col_i == tok_i, jnp.broadcast_to(routes[k : k + 1], (TOK, TOK)), 0.0),
            axis=1,
            keepdims=True,
        )
        for k in (0, 1)
    ]

    for d in (1, 2, 3):
        remote(
            st_s, st_r.at[d - 1], st_ss.at[d - 1], st_rs.at[d - 1], row_peers[d - 1]
        ).wait_recv()
    logs = [log_of(st_r[d - 1, TOK:PACK, :]) for d in (1, 2, 3)]
    states = [st_r[d - 1, 0:TOK, :].astype(F32) for d in (1, 2, 3)]
    zero = jnp.zeros_like(total)
    before = [(d <= x) for d in (1, 2, 3)]
    after_sum = sum((jnp.where(before[d], zero, logs[d]) for d in range(3)), zero)
    before_sum = sum((jnp.where(before[d], logs[d], zero) for d in range(3)), zero)
    prefix = jnp.zeros((TOK, HEAD), F32)
    row_total = jnp.exp(after_sum) * delta
    near, far = zero, zero
    for d in range(3):
        prefix = prefix + jnp.where(before[d], jnp.exp(near), zero) * states[d]
        reach = jnp.where(before[d], near + total + after_sum, far)
        row_total = row_total + jnp.exp(reach) * states[d]
        near = near + logs[d]
        far = far + jnp.where(before[d], zero, logs[d])
    rw_s[0:TOK, :] = row_total.astype(BF16)
    rw_s[TOK:PACK, :] = log_rows(total + before_sum + after_sum)
    s_in[...] = prefix

    rows_up = [
        remote(rw_s, rw_r.at[d - 1], rw_ss.at[d - 1], rw_rs.at[d - 1], col_peers[d - 1])
        for d in (1, 2)
    ]

    @pl.when(zl <= 1)
    def _():
        rows_up[0].start()

    @pl.when(zl == 0)
    def _():
        rows_up[1].start()

    @pl.when(zl >= 1)
    def _():
        rows_up[0].wait_recv()
        s_in[...] += jnp.exp(before_sum) * rw_r[0, 0:TOK, :].astype(F32)

    @pl.when(zl == 2)
    def _():
        rows_up[1].wait_recv()
        reach = before_sum + log_of(rw_r[0, TOK:PACK, :])
        s_in[...] += jnp.exp(reach) * rw_r[1, 0:TOK, :].astype(F32)

    state = s_in[...]
    state_high = state.astype(BF16)
    state_low = (state - state_high.astype(F32)).astype(BF16)
    inter = jnp.exp(cum_tok) * (dot(queries, state_high) + dot(queries, state_low)) / HEAD
    attended = intra + inter
    inverse_rms = lax.rsqrt(jnp.mean(attended * attended, axis=1, keepdims=True) + 1e-06)
    loads[4].wait()
    nb[:, 0:HEAD] = (attended * inverse_rms * gain_v[...].astype(F32)).astype(BF16)
    nb_copy = push(
        nb.at[:, 0:HEAD], nb.at[:, HEAD : 2 * HEAD], pr_ss.at[2], pr_rs.at[2], partner
    )
    loads[6].wait()
    wo_copy.wait_recv()
    nb_copy.wait_recv()

    def hop(piece, direction, left, send, recv, ssem, rsem):
        cols = cols_of(piece)
        return remote(
            send.at[direction, left - 1, :, cols],
            recv.at[direction, left - 1, :, cols],
            ssem.at[direction, left - 1, piece],
            rsem.at[direction, left - 1, piece],
            ynb[direction],
        )

    def reduce_rows(first, send, recv, ssem, rsem):
        def step(piece, direction, left, start):
            cols = cols_of(piece)
            target = (y + left) % NY if direction == 0 else (y + NY - left) % NY
            value = part[pl.ds(pl.multiple_of(target * CH, CH), CH), cols]
            if not start:
                hop(piece, direction, left + 1, send, recv, ssem, rsem).wait_recv()
                value = value + recv[direction, left, :, cols].astype(F32)
            send[direction, left - 1, :, cols] = value.astype(BF16)
            copy = hop(piece, direction, left, send, recv, ssem, rsem)
            copy.start()
            sent.append(copy)

        for piece in range(NP):
            part[:, cols_of(piece)] = first(piece)
            for direction in (0, 1):
                step(piece, direction, hops_of(piece)[direction], True)
        for t in (1, 2, 3):
            for piece in range(NP):
                for direction in (0, 1):
                    left = hops_of(piece)[direction] - t
                    if left >= 1:
                        step(piece, direction, left, False)
        for piece in range(NP):
            cols = cols_of(piece)
            value = part[pl.ds(pl.multiple_of(y * CH, CH), CH), cols]
            for direction in (0, 1):
                hop(piece, direction, 1, send, recv, ssem, rsem).wait_recv()
                value = value + recv[direction, 0, :, cols].astype(F32)
            yield piece, value

    heads = nb[...]

    def z_copy(piece, turn):
        first_a = (piece % 2 == 0) == (turn == 0)
        cols = cols_of(piece)
        return remote(
            z_s.at[turn, :, cols], z_r.at[turn, :, cols],
            z_ss.at[turn, piece], z_rs.at[turn, piece], za if first_a else zb,
        )

    def z_send(piece, turn, value):
        z_s[turn, :, cols_of(piece)] = value.astype(BF16)
        copy = z_copy(piece, turn)
        copy.start()
        sent.append(copy)

    for piece, value in reduce_rows(
        lambda piece: dot(heads, wo2[:, cols_of(piece)]), s1, r1, s1_ss, s1_rs
    ):
        acc_v[:, cols_of(piece)] = value
        z_send(piece, 0, value)
    for piece in range(NP):
        cols = cols_of(piece)
        z_copy(piece, 0).wait_recv()
        value = acc_v[:, cols] + z_r[0, :, cols].astype(F32)
        acc_v[:, cols] = value
        z_send(piece, 1, value)

    def place(chunk, core, piece):
        return mx.at[
            pl.ds(pl.multiple_of(chunk * CH, CH), CH),
            pl.ds(pl.multiple_of(core * HALF + piece * W, W), W),
        ]

    def ring(piece, direction, h):
        back = (y + NY - h) % NY if direction == 0 else (y + h) % NY
        return back

    def relay(piece, direction, h):
        chunk = ring(piece, direction, h - 1)
        spot = place(chunk, c, piece)
        return remote(
            spot, spot, ag_ss.at[direction, h - 1, piece], ag_rs.at[direction, h - 1, piece],
            ynb[direction],
        )

    def relayed(piece, direction, h):
        spot = place(ring(piece, direction, h), c, piece)
        return remote(
            spot, spot, ag_ss.at[direction, h - 1, piece], ag_rs.at[direction, h - 1, piece],
            ynb[direction],
        )

    def hand(piece, slot, chunk, core):
        spot = place(chunk, core, piece)
        return remote(spot, spot, pf_ss.at[slot, piece], pf_rs.at[slot, piece], partner)

    def start(copy):
        copy.start()
        sent.append(copy)

    handed = []
    for piece in range(NP):
        cols = cols_of(piece)
        z_copy(piece, 1).wait_recv()
        value = acc_v[:, cols] + z_r[1, :, cols].astype(F32)
        mx[
            pl.ds(pl.multiple_of(y * CH, CH), CH),
            pl.ds(pl.multiple_of(c * HALF + piece * W, W), W),
        ] = value.astype(BF16)
        for direction in (0, 1):
            start(relay(piece, direction, 1))
        start(hand(piece, 0, y, c))
        handed.append(hand(piece, 0, y, 1 - c))
    for h in (1, 2, 3, 4):
        for piece in range(NP):
            for direction in (0, 1):
                if h > hops_of(piece)[direction]:
                    continue
                relayed(piece, direction, h).wait_recv()
                if h < hops_of(piece)[direction]:
                    start(relay(piece, direction, h + 1))
                chunk = ring(piece, direction, h)
                slot = 1 + direction * 4 + h - 1
                start(hand(piece, slot, chunk, c))
                handed.append(hand(piece, slot, chunk, 1 - c))
    for copy in handed:
        copy.wait_recv()

    for i in (7, 8, 9, 10):
        loads[i].wait()
    mixed = mx[...]
    logits = dot_nt(mixed, rt_v[...])
    lane = lax.broadcasted_iota(jnp.int32, (TOK, EXPERTS), 1).astype(F32)
    member = (wanted[0] == lane) | (wanted[1] == lane)
    raised = jnp.where(member, jnp.exp(logits), 0.0)
    mine = jnp.sum(jnp.where(lane == zh.astype(F32), raised, 0.0), axis=1, keepdims=True)
    gate = mine / jnp.sum(raised, axis=1, keepdims=True)
    gate_part = dot_nt(mixed, wg_v[...])
    up_part = dot_nt(mixed, wu_v[...])
    hidden = gate_part / (1.0 + jnp.exp(-gate_part)) * up_part * gate
    hb[:, 0:FPAD] = jnp.zeros((TOK, FPAD), BF16)
    hb[:, 0:FFW] = hidden.astype(BF16)
    hb_copy = push(hb.at[:, 0:FPAD], hb.at[:, FPAD : 2 * FPAD], pr_ss.at[3], pr_rs.at[3], partner)
    wd_copy.wait_recv()
    hb_copy.wait_recv()
    units = hb[...]

    own_rows = lax.broadcasted_iota(jnp.int32, (CH, W), 0) // GR == zh
    for piece, value in reduce_rows(
        lambda piece: dot(units, wd2[:, cols_of(piece)]), s2, r2, s2_ss, s2_rs
    ):
        cols = cols_of(piece)
        rows = mx[
            pl.ds(pl.multiple_of(y * CH, CH), CH),
            pl.ds(pl.multiple_of(c * HALF + piece * W, W), W),
        ].astype(F32)
        value = value + jnp.where(own_rows, rows, 0.0)
        for g in range(NZH):
            group = value[g * GR : (g + 1) * GR, :]
            zh_acc[g, :, cols] = group
            zh_s[g, :, cols] = group.astype(BF16)

    zab_i = NZH - 1 - za_i
    firsts = [
        push(zh_s.at[za_i], zh_r.at[0], zh_ss.at[0], zh_rs.at[0], za),
        push(zh_s.at[zab_i], zh_r.at[1], zh_ss.at[1], zh_rs.at[1], za),
    ]
    firsts[1].wait_recv()
    fin_s[...] = (zh_acc[zb_i] + zh_r[1].astype(F32)).astype(BF16)
    second = push(fin_s, zh_r.at[2], zh_ss.at[2], zh_rs.at[2], zb)
    firsts[0].wait_recv()
    value = zh_acc[zh] + zh_r[0].astype(F32)
    second.wait_recv()
    value = (value + zh_r[2].astype(F32)).astype(BF16)
    fin_r[0] = value[0:2, :]
    fin_r[1] = value[2:4, :]
    last = push(fin_r.at[1 - c], fin_r.at[2], zh_ss.at[3], zh_rs.at[3], partner)
    out_ref[:, pl.ds(half, HALF)] = fin_r[c]
    last.wait_recv()
    out_ref[:, pl.ds(other, HALF)] = fin_r[2]

    for copy in sent:
        copy.wait_send()

    @pl.when(zl <= 1)
    def _():
        rows_up[0].wait_send()

    @pl.when(zl == 0)
    def _():
        rows_up[1].wait_send()


def layer(query, key_in, value, decay_log, norm_gain, w_out, router, routes, w_gate, w_up, w_down):
    dma = pltpu.SemaphoreType.DMA
    return pl.pallas_call(
        kernel,
        out_shape=jax.ShapeDtypeStruct((2, DM), BF16),
        in_specs=[pl.BlockSpec(memory_space=pl.ANY)] * 11,
        out_specs=pl.BlockSpec(memory_space=pltpu.VMEM),
        scratch_shapes=[
            pltpu.VMEM((TOK, HEAD), BF16),
            pltpu.VMEM((TOK, HEAD), BF16),
            pltpu.VMEM((TOK, HEAD), BF16),
            pltpu.VMEM((1, TOK), F32),
            pltpu.VMEM((1, HEAD), BF16),
            pltpu.VMEM((2 * HEAD, HALF), BF16),
            pltpu.VMEM((EXPERTS, DM), BF16),
            pltpu.VMEM((2, TOK), jnp.int32),
            pltpu.VMEM((FFW, DM), BF16),
            pltpu.VMEM((FFW, DM), BF16),
            pltpu.VMEM((2 * FPAD, HALF), BF16),
            pltpu.VMEM((PACK, HEAD), BF16),
            pltpu.VMEM((3, PACK, HEAD), BF16),
            pltpu.VMEM((PACK, HEAD), BF16),
            pltpu.VMEM((2, PACK, HEAD), BF16),
            pltpu.VMEM((TOK, HEAD), F32),
            pltpu.VMEM((TOK, 2 * HEAD), BF16),
            pltpu.VMEM((TOK, HALF), F32),
            pltpu.VMEM((2, 4, CH, HALF), BF16),
            pltpu.VMEM((2, 4, CH, HALF), BF16),
            pltpu.VMEM((CH, HALF), F32),
            pltpu.VMEM((2, CH, HALF), BF16),
            pltpu.VMEM((2, CH, HALF), BF16),
            pltpu.VMEM((TOK, DM), BF16),
            pltpu.VMEM((TOK, 2 * FPAD), BF16),
            pltpu.VMEM((2, 4, CH, HALF), BF16),
            pltpu.VMEM((2, 4, CH, HALF), BF16),
            pltpu.VMEM((NZH, GR, HALF), F32),
            pltpu.VMEM((NZH, GR, HALF), BF16),
            pltpu.VMEM((3, GR, HALF), BF16),
            pltpu.VMEM((GR, HALF), BF16),
            pltpu.VMEM((3, 2, HALF), BF16),
            dma((11,)),
            dma((3,)),
            dma((3,)),
            dma((2,)),
            dma((2,)),
            dma((4,)),
            dma((4,)),
            dma((2, 4, NP)),
            dma((2, 4, NP)),
            dma((2, NP)),
            dma((2, NP)),
            dma((2, 4, NP)),
            dma((2, 4, NP)),
            dma((9, NP)),
            dma((9, NP)),
            dma((2, 4, NP)),
            dma((2, 4, NP)),
            dma((4,)),
            dma((4,)),
        ],
        compiler_params=pltpu.CompilerParams(
            collective_id=0, has_side_effects=True, vmem_limit_bytes=56 << 20
        ),
        name="layer",
    )(
        query,
        key_in,
        value,
        decay_log.T,
        norm_gain.reshape(1, HEAD),
        w_out,
        router.T,
        routes.T,
        w_gate[0].T,
        w_up[0].T,
        w_down[0],
    )


def solution(mesh):
    placed = (
        P("seq", "exp"),
        P("seq", "exp"),
        P("seq", "exp"),
        P("seq", "exp"),
        P("exp"),
        P("exp", None),
        P(),
        P("seq", None),
        P("exp", None, None),
        P("exp", None, None),
        P("exp", None, None),
    )
    return jax.shard_map(
        layer, mesh=mesh, in_specs=placed, out_specs=P(("seq", "exp"), None), check_vma=False
    )
```

time: 1180 us -> 91.3 us (0.08)
  waiting for transfers between devices: 713 us -> 0 us
  blocking collectives: 390 us -> 0 us
  Pallas kernels: 0 us -> 88.8 us
  matrix products: 18.3 us -> 0 us
  local copies, waits for them, and re-layouts: 16.4 us -> 1.34 us
  between operations: 15 us -> 0.01 us
  other arithmetic: 14.2 us -> 0 us
    unnamed x3 -> x0, waiting for transfers between devices: 618 us -> none
    unnamed x2 -> x0, blocking collectives: 366 us -> none
    all_gather x1 -> x0, waiting for transfers between devices: 94.7 us -> none  [local(): mixed = lax.all_gather(own_mixed, 'exp', axis=0, tiled=True)]
    pallas_call x0 -> x1, Pallas kernels: none -> 88.8 us  [layer(): pl.pallas_call(kernel, out_shape=jax.ShapeDtypeStruct((2, DM), BF16), in_...]
    all_gather x1 -> x0, blocking collectives: 23.6 us -> none  [carried_in(): lax.all_gather(part.astype(kind), axis)]
    dot_general x9 -> x0, matrix products: 18.3 us -> none  [the longest x1 5.28 us: local(): slice_out = jnp.dot(hidden, w_down[0], preferred_element_type=jnp.float32)]
  transfers between devices with their start and end apart: 2 -> 0, of which waited for: 2 -> 0; matrix products, arithmetic and copies ran while one was open for 0% -> 0% of each run, Pallas kernels for 0% -> 0%
where the time goes in v1:
time: 91.3 us; the launch traced here: 90.1 us
  Pallas kernels  88.8 us (97%)
  local copies, waits for them, and re-layouts  1.34 us (1%)
    pallas_call x1, Pallas kernels, layer(): pl.pallas_call(kernel, out_shape=jax.ShapeDtypeStruct((2, DM), BF16), in_...  88.8 us

profile of v1, /device:TPU:1, one launch (start us, length us, event | category | flops | bytes accessed | tf_op | source)
XLA Modules:
  0.0 90.1 jit_solution(2199791841266295749)
XLA Ops:
  0.0 88.8 %layer.1 = bf16[2,4096]{1,0:T(2,128)(2,1)} custom-call(bf16[128,128]{1,0:T(8,128)(2,1)} %q_hbm.1, bf16[128,128]{1,0:T(8,128)(2,1)} %k_hbm.1, bf16[128,128]{1,0:T(8,128)(2,1)} %v_hbm.1, f32[1,128]{1,0:T(1,128)} %bitcast.16, bf16[1,128]{1,0:T(2,128)(2,1)} %bitcast.17, bf16[128,4096]{1,0:T(8,128)(2,1)} %wo_hbm.1, bf16[4,4096]{1,0:T(4,128)(2,1)} %bitcast.14, ...), custom_call_target="tpu_custom_call" | custom-call | tf_op jit(solution)/shard_map/layer/pallas_call | solution.py:439
  88.8 1.3 %copy.13 = bf16[2,4096]{1,0:T(2,128)(2,1)} copy(bf16[2,4096]{1,0:T(2,128)(2,1)} %layer.1) | data formatting | bytes 32768

commit v2 on v1

--- a/solution.py
+++ b/solution.py
@@ -14,13 +14,9 @@
 CH = TOK // NY
 GR = CH // NZH
 FPAD = 384
-NP = 4
+NP = 2
 W = HALF // NP
 PACK = TOK + 16
-
-
-def hops_of(piece):
-    return (4, 3) if piece % 2 == 0 else (3, 4)
 
 
 def cols_of(piece):
@@ -60,9 +56,9 @@
     out_ref,
     q_v, k_v, v_v, dec_v, gain_v, wo2, rt_v, routes_v, wg_v, wu_v, wd2,
     st_s, st_r, rw_s, rw_r, s_in, nb, part, s1, r1, acc_v, z_s, z_r, mx, hb, s2, r2,
-    zh_acc, zh_s, zh_r, fin_s, fin_r,
+    f_acc, f_s, f_r, f_own,
     ld, st_ss, st_rs, rw_ss, rw_rs, pr_ss, pr_rs, s1_ss, s1_rs, z_ss, z_rs, ag_ss, ag_rs, pf_ss, pf_rs,
-    s2_ss, s2_rs, zh_ss, zh_rs,
+    s2_ss, s2_rs, f_ss, f_rs,
 ):
     seq = lax.axis_index("seq")
     ex = lax.axis_index("exp")
@@ -78,13 +74,14 @@
     up = (seq, exp_id(zh, (y + 1) % NY, c))
     down = (seq, exp_id(zh, (y + NY - 1) % NY, c))
     ynb = (up, down)
+    ynb2 = [(seq, exp_id(zh, (y + d) % NY, c)) for d in (2, NY - 2)]
     za_i, zb_i = zh + 1 - 2 * (zh % 2), NZH - 1 - zh
     za, zb = (seq, exp_id(za_i, y, c)), (seq, exp_id(zb_i, y, c))
     row_peers = [(zl * NX + (x + d) % NX, ex) for d in (1, 2, 3)]
     col_peers = [(((zl + d) % NZL) * NX + x, ex) for d in (1, 2)]
 
     barrier = pltpu.get_barrier_semaphore()
-    peers = [partner, up, down, za, zb] + row_peers + col_peers
+    peers = [partner, up, down, za, zb] + ynb2 + row_peers + col_peers
     for peer in peers:
         pl.semaphore_signal(barrier, inc=1, device_id=peer, device_id_type=MESH)
 
@@ -119,11 +116,13 @@
 
     sent = []
 
-    def push(*args):
-        copy = remote(*args)
+    def start(copy):
         copy.start()
         sent.append(copy)
         return copy
+
+    def push(*args):
+        return start(remote(*args))
 
     row_i = lax.broadcasted_iota(jnp.int32, (TOK, TOK), 0)
     col_i = lax.broadcasted_iota(jnp.int32, (TOK, TOK), 1)
@@ -239,45 +238,53 @@
     wo_copy.wait_recv()
     nb_copy.wait_recv()
 
-    def hop(piece, direction, left, send, recv, ssem, rsem):
+    def span(piece, direction, role, send, recv, ssem, rsem):
         cols = cols_of(piece)
         return remote(
-            send.at[direction, left - 1, :, cols],
-            recv.at[direction, left - 1, :, cols],
-            ssem.at[direction, left - 1, piece],
-            rsem.at[direction, left - 1, piece],
-            ynb[direction],
+            send.at[direction, role, :, cols],
+            recv.at[direction, role, :, cols],
+            ssem.at[direction, role, piece],
+            rsem.at[direction, role, piece],
+            ynb[direction] if role in (0, 2) else ynb2[direction],
         )
 
+    def chunk_at(shift, cols):
+        return part[pl.ds(pl.multiple_of((y + NY + shift) % NY * CH, CH), CH), cols]
+
     def reduce_rows(first, send, recv, ssem, rsem):
-        def step(piece, direction, left, start):
-            cols = cols_of(piece)
-            target = (y + left) % NY if direction == 0 else (y + NY - left) % NY
-            value = part[pl.ds(pl.multiple_of(target * CH, CH), CH), cols]
-            if not start:
-                hop(piece, direction, left + 1, send, recv, ssem, rsem).wait_recv()
-                value = value + recv[direction, left, :, cols].astype(F32)
-            send[direction, left - 1, :, cols] = value.astype(BF16)
-            copy = hop(piece, direction, left, send, recv, ssem, rsem)
-            copy.start()
-            sent.append(copy)
-
-        for piece in range(NP):
-            part[:, cols_of(piece)] = first(piece)
-            for direction in (0, 1):
-                step(piece, direction, hops_of(piece)[direction], True)
-        for t in (1, 2, 3):
-            for piece in range(NP):
-                for direction in (0, 1):
-                    left = hops_of(piece)[direction] - t
-                    if left >= 1:
-                        step(piece, direction, left, False)
+        refs = (send, recv, ssem, rsem)
+        sign = (1, -1)
+
+        def give(piece, direction, role, value):
+            send[direction, role, :, cols_of(piece)] = value.astype(BF16)
+            start(span(piece, direction, role, *refs))
+
         for piece in range(NP):
             cols = cols_of(piece)
-            value = part[pl.ds(pl.multiple_of(y * CH, CH), CH), cols]
-            for direction in (0, 1):
-                hop(piece, direction, 1, send, recv, ssem, rsem).wait_recv()
-                value = value + recv[direction, 0, :, cols].astype(F32)
+            part[:, cols] = first(piece)
+            far = piece % 2
+            give(piece, far, 1, chunk_at(4, cols))
+            for d in (0, 1):
+                give(piece, d, 0, chunk_at(3 * sign[d], cols))
+        for piece in range(NP):
+            for d in (0, 1):
+                give(piece, d, 2, chunk_at(sign[d], cols_of(piece)))
+        for piece in range(NP):
+            cols = cols_of(piece)
+            for d in (1 - piece % 2, piece % 2):
+                value = chunk_at(2 * sign[d], cols)
+                roles = (0, 1) if d == piece % 2 else (0,)
+                for role in roles:
+                    span(piece, d, role, *refs).wait_recv()
+                    value = value + recv[d, role, :, cols].astype(F32)
+                give(piece, d, 3, value)
+        for piece in range(NP):
+            cols = cols_of(piece)
+            value = chunk_at(0, cols)
+            for role in (2, 3):
+                for d in (0, 1):
+                    span(piece, d, role, *refs).wait_recv()
+                    value = value + recv[d, role, :, cols].astype(F32)
             yield piece, value
 
     heads = nb[...]
@@ -292,9 +299,7 @@
 
     def z_send(piece, turn, value):
         z_s[turn, :, cols_of(piece)] = value.astype(BF16)
-        copy = z_copy(piece, turn)
-        copy.start()
-        sent.append(copy)
+        start(z_copy(piece, turn))
 
     for piece, value in reduce_rows(
         lambda piece: dot(heads, wo2[:, cols_of(piece)]), s1, r1, s1_ss, s1_rs
@@ -314,34 +319,26 @@
             pl.ds(pl.multiple_of(core * HALF + piece * W, W), W),
         ]
 
-    def ring(piece, direction, h):
-        back = (y + NY - h) % NY if direction == 0 else (y + h) % NY
-        return back
-
-    def relay(piece, direction, h):
-        chunk = ring(piece, direction, h - 1)
+    def relay(piece, direction, far, chunk):
         spot = place(chunk, c, piece)
+        to = ynb[direction] if far in (1, 3) else ynb2[direction]
         return remote(
-            spot, spot, ag_ss.at[direction, h - 1, piece], ag_rs.at[direction, h - 1, piece],
-            ynb[direction],
+            spot, spot, ag_ss.at[direction, far - 1, piece], ag_rs.at[direction, far - 1, piece], to
         )
 
-    def relayed(piece, direction, h):
-        spot = place(ring(piece, direction, h), c, piece)
-        return remote(
-            spot, spot, ag_ss.at[direction, h - 1, piece], ag_rs.at[direction, h - 1, piece],
-            ynb[direction],
-        )
+    def origin(direction, far):
+        return (y + NY - far) % NY if direction == 0 else (y + far) % NY
 
     def hand(piece, slot, chunk, core):
         spot = place(chunk, core, piece)
         return remote(spot, spot, pf_ss.at[slot, piece], pf_rs.at[slot, piece], partner)
 
-    def start(copy):
-        copy.start()
-        sent.append(copy)
-
     handed = []
+
+    def pass_on(piece, slot, chunk):
+        start(hand(piece, slot, chunk, c))
+        handed.append(hand(piece, slot, chunk, 1 - c))
+
     for piece in range(NP):
         cols = cols_of(piece)
         z_copy(piece, 1).wait_recv()
@@ -350,36 +347,48 @@
             pl.ds(pl.multiple_of(y * CH, CH), CH),
             pl.ds(pl.multiple_of(c * HALF + piece * W, W), W),
         ] = value.astype(BF16)
-        for direction in (0, 1):
-            start(relay(piece, direction, 1))
-        start(hand(piece, 0, y, c))
-        handed.append(hand(piece, 0, y, 1 - c))
-    for h in (1, 2, 3, 4):
+        for far in (2, 1):
+            for direction in (0, 1):
+                start(relay(piece, direction, far, y))
+        pass_on(piece, 0, y)
+
+    def take(piece, direction, far):
+        chunk = origin(direction, far)
+        relay(piece, direction, far, chunk).wait_recv()
+        return chunk
+
+    for piece in range(NP):
+        for direction in (piece % 2, 1 - piece % 2):
+            chunk = take(piece, direction, 2)
+            if direction == piece % 2:
+                start(relay(piece, direction, 4, chunk))
+            start(relay(piece, direction, 3, chunk))
+            pass_on(piece, 1 + direction * 4 + 1, chunk)
+    for far in (1, 3, 4):
         for piece in range(NP):
             for direction in (0, 1):
-                if h > hops_of(piece)[direction]:
+                if far == 4 and direction != piece % 2:
                     continue
-                relayed(piece, direction, h).wait_recv()
-                if h < hops_of(piece)[direction]:
-                    start(relay(piece, direction, h + 1))
-                chunk = ring(piece, direction, h)
-                slot = 1 + direction * 4 + h - 1
-                start(hand(piece, slot, chunk, c))
-                handed.append(hand(piece, slot, chunk, 1 - c))
+                chunk = take(piece, direction, far)
+                pass_on(piece, 1 + direction * 4 + far - 1, chunk)
+
+    for i in (7, 8, 9, 10):
+        loads[i].wait()
+
+    def products(columns):
+        rows = mx[:, columns]
+        return [dot_nt(rows, ref[:, columns]) for ref in (rt_v, wg_v, wu_v)]
+
+    own_terms = products(pl.ds(half, HALF))
     for copy in handed:
         copy.wait_recv()
-
-    for i in (7, 8, 9, 10):
-        loads[i].wait()
-    mixed = mx[...]
-    logits = dot_nt(mixed, rt_v[...])
+    other_terms = products(pl.ds(other, HALF))
+    logits, gate_part, up_part = [a + b for a, b in zip(own_terms, other_terms)]
     lane = lax.broadcasted_iota(jnp.int32, (TOK, EXPERTS), 1).astype(F32)
     member = (wanted[0] == lane) | (wanted[1] == lane)
     raised = jnp.where(member, jnp.exp(logits), 0.0)
     mine = jnp.sum(jnp.where(lane == zh.astype(F32), raised, 0.0), axis=1, keepdims=True)
     gate = mine / jnp.sum(raised, axis=1, keepdims=True)
-    gate_part = dot_nt(mixed, wg_v[...])
-    up_part = dot_nt(mixed, wu_v[...])
     hidden = gate_part / (1.0 + jnp.exp(-gate_part)) * up_part * gate
     hb[:, 0:FPAD] = jnp.zeros((TOK, FPAD), BF16)
     hb[:, 0:FFW] = hidden.astype(BF16)
@@ -399,28 +408,31 @@
         ].astype(F32)
         value = value + jnp.where(own_rows, rows, 0.0)
         for g in range(NZH):
-            group = value[g * GR : (g + 1) * GR, :]
-            zh_acc[g, :, cols] = group
-            zh_s[g, :, cols] = group.astype(BF16)
-
-    zab_i = NZH - 1 - za_i
-    firsts = [
-        push(zh_s.at[za_i], zh_r.at[0], zh_ss.at[0], zh_rs.at[0], za),
-        push(zh_s.at[zab_i], zh_r.at[1], zh_ss.at[1], zh_rs.at[1], za),
-    ]
-    firsts[1].wait_recv()
-    fin_s[...] = (zh_acc[zb_i] + zh_r[1].astype(F32)).astype(BF16)
-    second = push(fin_s, zh_r.at[2], zh_ss.at[2], zh_rs.at[2], zb)
-    firsts[0].wait_recv()
-    value = zh_acc[zh] + zh_r[0].astype(F32)
-    second.wait_recv()
-    value = (value + zh_r[2].astype(F32)).astype(BF16)
-    fin_r[0] = value[0:2, :]
-    fin_r[1] = value[2:4, :]
-    last = push(fin_r.at[1 - c], fin_r.at[2], zh_ss.at[3], zh_rs.at[3], partner)
-    out_ref[:, pl.ds(half, HALF)] = fin_r[c]
-    last.wait_recv()
-    out_ref[:, pl.ds(other, HALF)] = fin_r[2]
+            for k in (0, 1):
+                rows = value[g * GR + 2 * k : g * GR + 2 * k + 2, :]
+                f_acc[g, k, :, cols] = rows
+                f_s[g, k, :, cols] = rows.astype(BF16)
+
+    for d in (2, 1, 3):
+        to = (zh + d) % NZH
+        for k in (0, 1):
+            push(
+                f_s.at[to, k], f_r.at[d - 1, c], f_ss.at[d - 1, k], f_rs.at[d - 1, c],
+                (seq, exp_id(to, y, k)),
+            )
+    push(f_acc.at[zh, 1 - c], f_own.at[c], f_ss.at[3, 0], f_rs.at[3, 0], partner)
+    f_own[c] = f_acc[zh, c]
+    remote(f_acc.at[zh, 1 - c], f_own.at[1 - c], f_ss.at[3, 0], f_rs.at[3, 0], partner).wait_recv()
+    for d in (1, 3, 2):
+        for k in (0, 1):
+            remote(
+                f_s.at[0, k], f_r.at[d - 1, k], f_ss.at[d - 1, k], f_rs.at[d - 1, k], partner
+            ).wait_recv()
+    for k in (0, 1):
+        value = f_own[k]
+        for d in range(3):
+            value = value + f_r[d, k].astype(F32)
+        out_ref[:, k * HALF : (k + 1) * HALF] = value.astype(BF16)
 
     for copy in sent:
         copy.wait_send()
@@ -469,11 +481,10 @@
             pltpu.VMEM((TOK, 2 * FPAD), BF16),
             pltpu.VMEM((2, 4, CH, HALF), BF16),
             pltpu.VMEM((2, 4, CH, HALF), BF16),
-            pltpu.VMEM((NZH, GR, HALF), F32),
-            pltpu.VMEM((NZH, GR, HALF), BF16),
-            pltpu.VMEM((3, GR, HALF), BF16),
-            pltpu.VMEM((GR, HALF), BF16),
-            pltpu.VMEM((3, 2, HALF), BF16),
+            pltpu.VMEM((NZH, 2, 2, HALF), F32),
+            pltpu.VMEM((NZH, 2, 2, HALF), BF16),
+            pltpu.VMEM((3, 2, 2, HALF), BF16),
+            pltpu.VMEM((2, 2, HALF), F32),
             dma((11,)),
             dma((3,)),
             dma((3,)),
@@ -491,8 +502,8 @@
             dma((9, NP)),
             dma((2, 4, NP)),
             dma((2, 4, NP)),
-            dma((4,)),
-            dma((4,)),
+            dma((4, 2)),
+            dma((4, 2)),
         ],
         compiler_params=pltpu.CompilerParams(
             collective_id=0, has_side_effects=True, vmem_limit_bytes=56 << 20

time: 91.3 us -> 75.6 us (0.83); the launches traced: 90.1 us -> 75.4 us
  Pallas kernels: 88.8 us -> 74.1 us
    pallas_call x1, Pallas kernels: 88.8 us -> 74.1 us  [layer(): pl.pallas_call(kernel, out_shape=jax.ShapeDtypeStruct((2, DM), BF16), in_...]
where the time goes in v2:
time: 75.6 us; the launch traced here: 75.4 us
  Pallas kernels  74.1 us (98%)
  local copies, waits for them, and re-layouts  1.34 us (2%)
    pallas_call x1, Pallas kernels, layer(): pl.pallas_call(kernel, out_shape=jax.ShapeDtypeStruct((2, DM), BF16), in_...  74.1 us

profile of v2, /device:TPU:1, one launch (start us, length us, event | category | flops | bytes accessed | tf_op | source)
XLA Modules:
  0.0 75.4 jit_solution(8420303707414811866)
XLA Ops:
  0.0 74.1 %layer.1 = bf16[2,4096]{1,0:T(2,128)(2,1)} custom-call(bf16[128,128]{1,0:T(8,128)(2,1)} %q_hbm.1, bf16[128,128]{1,0:T(8,128)(2,1)} %k_hbm.1, bf16[128,128]{1,0:T(8,128)(2,1)} %v_hbm.1, f32[1,128]{1,0:T(1,128)} %bitcast.16, bf16[1,128]{1,0:T(2,128)(2,1)} %bitcast.17, bf16[128,4096]{1,0:T(8,128)(2,1)} %wo_hbm.1, bf16[4,4096]{1,0:T(4,128)(2,1)} %bitcast.14, ...), custom_call_target="tpu_custom_call" | custom-call | tf_op jit(solution)/shard_map/layer/pallas_call | solution.py:451
  74.1 1.3 %copy.13 = bf16[2,4096]{1,0:T(2,128)(2,1)} copy(bf16[2,4096]{1,0:T(2,128)(2,1)} %layer.1) | data formatting | bytes 32768

commit v3 on v2

--- a/solution.py
+++ b/solution.py
@@ -14,7 +14,7 @@
 CH = TOK // NY
 GR = CH // NZH
 FPAD = 384
-NP = 2
+NP = 4
 W = HALF // NP
 PACK = TOK + 16
 
@@ -80,20 +80,15 @@
     row_peers = [(zl * NX + (x + d) % NX, ex) for d in (1, 2, 3)]
     col_peers = [(((zl + d) % NZL) * NX + x, ex) for d in (1, 2)]
 
-    barrier = pltpu.get_barrier_semaphore()
-    peers = [partner, up, down, za, zb] + ynb2 + row_peers + col_peers
-    for peer in peers:
-        pl.semaphore_signal(barrier, inc=1, device_id=peer, device_id_type=MESH)
-
     half = pl.multiple_of(c * HALF, HALF)
     other = pl.multiple_of((1 - c) * HALF, HALF)
     loads = [
         pltpu.make_async_copy(src, dst, ld.at[i])
         for i, (src, dst) in enumerate(
             [
+                (dec_hbm, dec_v),
                 (k_hbm, k_v),
                 (v_hbm, v_v),
-                (dec_hbm, dec_v),
                 (q_hbm, q_v),
                 (gain_hbm, gain_v),
                 (routes_hbm, routes_v),
@@ -105,7 +100,13 @@
             ]
         )
     ]
-    for load in loads:
+    for load in loads[:3]:
+        load.start()
+    barrier = pltpu.get_barrier_semaphore()
+    peers = [partner, up, down, za, zb] + ynb2 + row_peers + col_peers
+    for peer in peers:
+        pl.semaphore_signal(barrier, inc=1, device_id=peer, device_id_type=MESH)
+    for load in loads[3:]:
         load.start()
 
     def remote(src, dst, send, recv, device):
@@ -128,25 +129,21 @@
     col_i = lax.broadcasted_iota(jnp.int32, (TOK, TOK), 1)
     tok_i = (row_i % CH) // GR * (NY * GR) + row_i // CH * GR + row_i % GR
 
-    loads[2].wait()
+    loads[0].wait()
     dec_row = dec_v[...]
     dec_full = jnp.broadcast_to(dec_row, (TOK, TOK))
-    dec_col = jnp.sum(jnp.where(row_i == col_i, dec_full, 0.0), axis=1, keepdims=True)
-    cum_row = jnp.sum(jnp.where(row_i <= col_i, dec_col, 0.0), axis=0, keepdims=True)
-    cum_col = jnp.sum(jnp.where(col_i <= row_i, dec_full, 0.0), axis=1, keepdims=True)
-    cum_tok = jnp.sum(jnp.where(col_i <= tok_i, dec_full, 0.0), axis=1, keepdims=True)
+    tail = jnp.exp(jnp.sum(jnp.where(col_i > row_i, dec_full, 0.0), axis=1, keepdims=True))
     total = jnp.broadcast_to(jnp.sum(dec_row, axis=1, keepdims=True), (1, HEAD))
-    loads[0].wait()
+    st_s[TOK:PACK, :] = log_rows(total)
     loads[1].wait()
-    tail = jnp.exp(total[:, 0:1] - cum_col)
+    loads[2].wait()
     keys = k_v[...]
     values = v_v[...]
     delta = dot_tn((keys.astype(F32) * tail).astype(BF16), values)
     st_s[0:TOK, :] = delta.astype(BF16)
-    st_s[TOK:PACK, :] = log_rows(total)
 
     pl.semaphore_wait(barrier, len(peers))
-    for d in (1, 2, 3):
+    for d in (2, 1, 3):
         push(st_s, st_r.at[d - 1], st_ss.at[d - 1], st_rs.at[d - 1], row_peers[d - 1])
     wo_copy = push(
         wo_hbm.at[:, pl.ds(other, HALF)], wo2.at[HEAD : 2 * HEAD], pr_ss.at[0], pr_rs.at[0], partner
@@ -157,6 +154,9 @@
     wd2[FFW:FPAD, :] = jnp.zeros((FPAD - FFW, HALF), BF16)
     wd2[FPAD + FFW : 2 * FPAD, :] = jnp.zeros((FPAD - FFW, HALF), BF16)
 
+    dec_col = jnp.sum(jnp.where(row_i == col_i, dec_full, 0.0), axis=1, keepdims=True)
+    cum_row = jnp.sum(jnp.where(row_i <= col_i, dec_col, 0.0), axis=0, keepdims=True)
+    cum_tok = jnp.sum(jnp.where(col_i <= tok_i, dec_full, 0.0), axis=1, keepdims=True)
     loads[3].wait()
     to_rows = jnp.where(col_i == tok_i, 1.0, 0.0).astype(BF16)
     queries = dot(to_rows, q_v[...]).astype(BF16)
@@ -239,13 +239,13 @@
     nb_copy.wait_recv()
 
     def span(piece, direction, role, send, recv, ssem, rsem):
-        cols = cols_of(piece)
+        cols = slice(0, HALF) if role == 3 else cols_of(piece)
         return remote(
             send.at[direction, role, :, cols],
             recv.at[direction, role, :, cols],
             ssem.at[direction, role, piece],
             rsem.at[direction, role, piece],
-            ynb[direction] if role in (0, 2) else ynb2[direction],
+            ynb[direction] if role in (0, 3) else ynb2[direction],
         )
 
     def chunk_at(shift, cols):
@@ -266,9 +266,9 @@
             give(piece, far, 1, chunk_at(4, cols))
             for d in (0, 1):
                 give(piece, d, 0, chunk_at(3 * sign[d], cols))
-        for piece in range(NP):
-            for d in (0, 1):
-                give(piece, d, 2, chunk_at(sign[d], cols_of(piece)))
+        for d in (0, 1):
+            send[d, 3] = chunk_at(sign[d], slice(0, HALF)).astype(BF16)
+            start(span(0, d, 3, *refs))
         for piece in range(NP):
             cols = cols_of(piece)
             for d in (1 - piece % 2, piece % 2):
@@ -277,13 +277,14 @@
                 for role in roles:
                     span(piece, d, role, *refs).wait_recv()
                     value = value + recv[d, role, :, cols].astype(F32)
-                give(piece, d, 3, value)
+                give(piece, d, 2, value)
         for piece in range(NP):
             cols = cols_of(piece)
             value = chunk_at(0, cols)
-            for role in (2, 3):
+            for role in (3, 2):
                 for d in (0, 1):
-                    span(piece, d, role, *refs).wait_recv()
+                    if role == 2 or piece == 0:
+                        span(piece, d, role, *refs).wait_recv()
                     value = value + recv[d, role, :, cols].astype(F32)
             yield piece, value
 
@@ -319,25 +320,32 @@
             pl.ds(pl.multiple_of(core * HALF + piece * W, W), W),
         ]
 
+    def whole(chunk, core):
+        return mx.at[
+            pl.ds(pl.multiple_of(chunk * CH, CH), CH), pl.ds(pl.multiple_of(core * HALF, HALF), HALF)
+        ]
+
     def relay(piece, direction, far, chunk):
-        spot = place(chunk, c, piece)
+        spot = whole(chunk, c) if far == 1 else place(chunk, c, piece)
         to = ynb[direction] if far in (1, 3) else ynb2[direction]
         return remote(
             spot, spot, ag_ss.at[direction, far - 1, piece], ag_rs.at[direction, far - 1, piece], to
         )
 
-    def origin(direction, far):
-        return (y + NY - far) % NY if direction == 0 else (y + far) % NY
-
-    def hand(piece, slot, chunk, core):
-        spot = place(chunk, core, piece)
-        return remote(spot, spot, pf_ss.at[slot, piece], pf_rs.at[slot, piece], partner)
+    def take(piece, direction, far):
+        chunk = (y + NY - far) % NY if direction == 0 else (y + far) % NY
+        relay(piece, direction, far, chunk).wait_recv()
+        return chunk
+
+    def hand(slot, chunk, core):
+        spot = whole(chunk, core)
+        return remote(spot, spot, pf_ss.at[slot], pf_rs.at[slot], partner)
 
     handed = []
 
-    def pass_on(piece, slot, chunk):
-        start(hand(piece, slot, chunk, c))
-        handed.append(hand(piece, slot, chunk, 1 - c))
+    def pass_on(slot, chunk):
+        start(hand(slot, chunk, c))
+        handed.append(hand(slot, chunk, 1 - c))
 
     for piece in range(NP):
         cols = cols_of(piece)
@@ -347,30 +355,28 @@
             pl.ds(pl.multiple_of(y * CH, CH), CH),
             pl.ds(pl.multiple_of(c * HALF + piece * W, W), W),
         ] = value.astype(BF16)
-        for far in (2, 1):
-            for direction in (0, 1):
-                start(relay(piece, direction, far, y))
-        pass_on(piece, 0, y)
-
-    def take(piece, direction, far):
-        chunk = origin(direction, far)
-        relay(piece, direction, far, chunk).wait_recv()
-        return chunk
-
+        for direction in (0, 1):
+            start(relay(piece, direction, 2, y))
+    for direction in (0, 1):
+        start(relay(0, direction, 1, y))
+    pass_on(0, y)
     for piece in range(NP):
         for direction in (piece % 2, 1 - piece % 2):
             chunk = take(piece, direction, 2)
             if direction == piece % 2:
                 start(relay(piece, direction, 4, chunk))
             start(relay(piece, direction, 3, chunk))
-            pass_on(piece, 1 + direction * 4 + 1, chunk)
-    for far in (1, 3, 4):
+            if piece == NP - 1:
+                pass_on(1 + direction, chunk)
+    for direction in (0, 1):
+        pass_on(3 + direction, take(0, direction, 1))
+    for direction in (0, 1):
         for piece in range(NP):
-            for direction in (0, 1):
-                if far == 4 and direction != piece % 2:
-                    continue
-                chunk = take(piece, direction, far)
-                pass_on(piece, 1 + direction * 4 + far - 1, chunk)
+            chunk = take(piece, direction, 3)
+        pass_on(5 + direction, chunk)
+    for piece in range(NP):
+        chunk = take(piece, piece % 2, 4)
+    pass_on(7, chunk)
 
     for i in (7, 8, 9, 10):
         loads[i].wait()
@@ -413,6 +419,7 @@
                 f_acc[g, k, :, cols] = rows
                 f_s[g, k, :, cols] = rows.astype(BF16)
 
+    earlier, sent[:] = list(sent), []
     for d in (2, 1, 3):
         to = (zh + d) % NZH
         for k in (0, 1):
@@ -422,6 +429,17 @@
             )
     push(f_acc.at[zh, 1 - c], f_own.at[c], f_ss.at[3, 0], f_rs.at[3, 0], partner)
     f_own[c] = f_acc[zh, c]
+    for copy in earlier:
+        copy.wait_send()
+
+    @pl.when(zl <= 1)
+    def _():
+        rows_up[0].wait_send()
+
+    @pl.when(zl == 0)
+    def _():
+        rows_up[1].wait_send()
+
     remote(f_acc.at[zh, 1 - c], f_own.at[1 - c], f_ss.at[3, 0], f_rs.at[3, 0], partner).wait_recv()
     for d in (1, 3, 2):
         for k in (0, 1):
@@ -437,20 +455,12 @@
     for copy in sent:
         copy.wait_send()
 
-    @pl.when(zl <= 1)
-    def _():
-        rows_up[0].wait_send()
-
-    @pl.when(zl == 0)
-    def _():
-        rows_up[1].wait_send()
-
 
 def layer(query, key_in, value, decay_log, norm_gain, w_out, router, routes, w_gate, w_up, w_down):
     dma = pltpu.SemaphoreType.DMA
     return pl.pallas_call(
         kernel,
-        out_shape=jax.ShapeDtypeStruct((2, DM), BF16),
+        out_shape=pltpu.VMEM((2, DM), BF16),
         in_specs=[pl.BlockSpec(memory_space=pl.ANY)] * 11,
         out_specs=pl.BlockSpec(memory_space=pltpu.VMEM),
         scratch_shapes=[
@@ -498,8 +508,8 @@
             dma((2, NP)),
             dma((2, 4, NP)),
             dma((2, 4, NP)),
-            dma((9, NP)),
-            dma((9, NP)),
+            dma((8,)),
+            dma((8,)),
             dma((2, 4, NP)),
             dma((2, 4, NP)),
             dma((4, 2)),

time: 75.6 us -> 72.7 us (0.962)
  Pallas kernels: 74.1 us -> 71.9 us
    pallas_call x1, Pallas kernels: 74.1 us -> 71.9 us  [layer(): pl.pallas_call(kernel, out_shape=pltpu.VMEM((2, DM), BF16), in_specs=[pl....]
where the time goes in v3:
time: 72.7 us; the launch traced here: 72.5 us
  Pallas kernels  71.9 us (99%)
    pallas_call x1, Pallas kernels, layer(): pl.pallas_call(kernel, out_shape=pltpu.VMEM((2, DM), BF16), in_specs=[pl....  71.9 us

profile of v3, /device:TPU:1, one launch (start us, length us, event | category | flops | bytes accessed | tf_op | source)
XLA Modules:
  0.0 72.5 jit_solution(6180070771699191510)
XLA Ops:
  0.0 71.9 %layer.1 = bf16[2,4096]{1,0:T(2,128)(2,1)S(1)} custom-call(bf16[128,128]{1,0:T(8,128)(2,1)} %q_hbm.1, bf16[128,128]{1,0:T(8,128)(2,1)} %k_hbm.1, bf16[128,128]{1,0:T(8,128)(2,1)} %v_hbm.1, f32[1,128]{1,0:T(1,128)} %bitcast.16, bf16[1,128]{1,0:T(2,128)(2,1)} %bitcast.17, bf16[128,4096]{1,0:T(8,128)(2,1)} %wo_hbm.1, bf16[4,4096]{1,0:T(4,128)(2,1)} %bitcast.14, ...), custom_call_target="tpu_custom_call" | custom-call | tf_op jit(solution)/shard_map/layer/pallas_call | solution.py:461
  71.9 0.6 copy.13

commit v4 on v3

--- a/solution.py
+++ b/solution.py
@@ -151,30 +151,6 @@
     wd_copy = push(
         wd_hbm.at[:, pl.ds(other, HALF)], wd2.at[FPAD : FPAD + FFW], pr_ss.at[1], pr_rs.at[1], partner
     )
-    wd2[FFW:FPAD, :] = jnp.zeros((FPAD - FFW, HALF), BF16)
-    wd2[FPAD + FFW : 2 * FPAD, :] = jnp.zeros((FPAD - FFW, HALF), BF16)
-
-    dec_col = jnp.sum(jnp.where(row_i == col_i, dec_full, 0.0), axis=1, keepdims=True)
-    cum_row = jnp.sum(jnp.where(row_i <= col_i, dec_col, 0.0), axis=0, keepdims=True)
-    cum_tok = jnp.sum(jnp.where(col_i <= tok_i, dec_full, 0.0), axis=1, keepdims=True)
-    loads[3].wait()
-    to_rows = jnp.where(col_i == tok_i, 1.0, 0.0).astype(BF16)
-    queries = dot(to_rows, q_v[...]).astype(BF16)
-    causal = col_i <= tok_i
-    scores = dot_nt(queries, keys)
-    weights = jnp.where(causal, jnp.exp(jnp.where(causal, cum_tok - cum_row, 0.0)), 0.0)
-    intra = dot((scores * weights / HEAD).astype(BF16), values)
-
-    loads[5].wait()
-    routes = routes_v[...].astype(F32)
-    wanted = [
-        jnp.sum(
-            jnp.where(col_i == tok_i, jnp.broadcast_to(routes[k : k + 1], (TOK, TOK)), 0.0),
-            axis=1,
-            keepdims=True,
-        )
-        for k in (0, 1)
-    ]
 
     for d in (1, 2, 3):
         remote(
@@ -211,6 +187,17 @@
     @pl.when(zl == 0)
     def _():
         rows_up[1].start()
+
+    dec_col = jnp.sum(jnp.where(row_i == col_i, dec_full, 0.0), axis=1, keepdims=True)
+    cum_row = jnp.sum(jnp.where(row_i <= col_i, dec_col, 0.0), axis=0, keepdims=True)
+    cum_tok = jnp.sum(jnp.where(col_i <= tok_i, dec_full, 0.0), axis=1, keepdims=True)
+    loads[3].wait()
+    to_rows = jnp.where(col_i == tok_i, 1.0, 0.0).astype(BF16)
+    queries = dot(to_rows, q_v[...]).astype(BF16)
+    causal = col_i <= tok_i
+    scores = dot_nt(queries, keys)
+    weights = jnp.where(causal, jnp.exp(jnp.where(causal, cum_tok - cum_row, 0.0)), 0.0)
+    intra = dot((scores * weights / HEAD).astype(BF16), values)
 
     @pl.when(zl >= 1)
     def _():
@@ -307,6 +294,11 @@
     ):
         acc_v[:, cols_of(piece)] = value
         z_send(piece, 0, value)
+    loads[5].wait()
+    wanted = dot_nt(routes_v[...].astype(BF16), to_rows)
+    wd2[FFW:FPAD, :] = jnp.zeros((FPAD - FFW, HALF), BF16)
+    wd2[FPAD + FFW : 2 * FPAD, :] = jnp.zeros((FPAD - FFW, HALF), BF16)
+
     for piece in range(NP):
         cols = cols_of(piece)
         z_copy(piece, 0).wait_recv()
@@ -383,19 +375,19 @@
 
     def products(columns):
         rows = mx[:, columns]
-        return [dot_nt(rows, ref[:, columns]) for ref in (rt_v, wg_v, wu_v)]
+        return [dot_nt(ref[:, columns], rows) for ref in (rt_v, wg_v, wu_v)]
 
     own_terms = products(pl.ds(half, HALF))
     for copy in handed:
         copy.wait_recv()
     other_terms = products(pl.ds(other, HALF))
     logits, gate_part, up_part = [a + b for a, b in zip(own_terms, other_terms)]
-    lane = lax.broadcasted_iota(jnp.int32, (TOK, EXPERTS), 1).astype(F32)
-    member = (wanted[0] == lane) | (wanted[1] == lane)
+    expert = lax.broadcasted_iota(jnp.int32, (EXPERTS, TOK), 0).astype(F32)
+    member = (wanted[0:1] == expert) | (wanted[1:2] == expert)
     raised = jnp.where(member, jnp.exp(logits), 0.0)
-    mine = jnp.sum(jnp.where(lane == zh.astype(F32), raised, 0.0), axis=1, keepdims=True)
-    gate = mine / jnp.sum(raised, axis=1, keepdims=True)
-    hidden = gate_part / (1.0 + jnp.exp(-gate_part)) * up_part * gate
+    mine = jnp.sum(jnp.where(expert == zh.astype(F32), raised, 0.0), axis=0, keepdims=True)
+    gate = mine / jnp.sum(raised, axis=0, keepdims=True)
+    hidden = (gate_part / (1.0 + jnp.exp(-gate_part)) * up_part * gate).T
     hb[:, 0:FPAD] = jnp.zeros((TOK, FPAD), BF16)
     hb[:, 0:FFW] = hidden.astype(BF16)
     hb_copy = push(hb.at[:, 0:FPAD], hb.at[:, FPAD : 2 * FPAD], pr_ss.at[3], pr_rs.at[3], partner)

time: 72.7 us -> 72.7 us (level)
  no operation moved by 1% of the time
where the time goes in v4:
time: 72.7 us; the launch traced here: 72.5 us
  Pallas kernels  71.9 us (99%)
    pallas_call x1, Pallas kernels, layer(): pl.pallas_call(kernel, out_shape=pltpu.VMEM((2, DM), BF16), in_specs=[pl....  71.9 us

profile of v4, /device:TPU:1, one launch (start us, length us, event | category | flops | bytes accessed | tf_op | source)
XLA Modules:
  0.0 72.5 jit_solution(5158776420581739886)
XLA Ops:
  0.0 71.9 %layer.1 = bf16[2,4096]{1,0:T(2,128)(2,1)S(1)} custom-call(bf16[128,128]{1,0:T(8,128)(2,1)} %q_hbm.1, bf16[128,128]{1,0:T(8,128)(2,1)} %k_hbm.1, bf16[128,128]{1,0:T(8,128)(2,1)} %v_hbm.1, f32[1,128]{1,0:T(1,128)} %bitcast.16, bf16[1,128]{1,0:T(2,128)(2,1)} %bitcast.17, bf16[128,4096]{1,0:T(8,128)(2,1)} %wo_hbm.1, bf16[4,4096]{1,0:T(4,128)(2,1)} %bitcast.14, ...), custom_call_target="tpu_custom_call" | custom-call | tf_op jit(solution)/shard_map/layer/pallas_call | solution.py:453
  71.9 0.6 copy.13

commit v5 on v4

--- a/solution.py
+++ b/solution.py
@@ -296,6 +296,7 @@
         z_send(piece, 0, value)
     loads[5].wait()
     wanted = dot_nt(routes_v[...].astype(BF16), to_rows)
+    hb[:, 0:FPAD] = jnp.zeros((TOK, FPAD), BF16)
     wd2[FFW:FPAD, :] = jnp.zeros((FPAD - FFW, HALF), BF16)
     wd2[FPAD + FFW : 2 * FPAD, :] = jnp.zeros((FPAD - FFW, HALF), BF16)
 
@@ -355,9 +356,9 @@
     for piece in range(NP):
         for direction in (piece % 2, 1 - piece % 2):
             chunk = take(piece, direction, 2)
+            start(relay(piece, direction, 3, chunk))
             if direction == piece % 2:
                 start(relay(piece, direction, 4, chunk))
-            start(relay(piece, direction, 3, chunk))
             if piece == NP - 1:
                 pass_on(1 + direction, chunk)
     for direction in (0, 1):
@@ -388,7 +389,6 @@
     mine = jnp.sum(jnp.where(expert == zh.astype(F32), raised, 0.0), axis=0, keepdims=True)
     gate = mine / jnp.sum(raised, axis=0, keepdims=True)
     hidden = (gate_part / (1.0 + jnp.exp(-gate_part)) * up_part * gate).T
-    hb[:, 0:FPAD] = jnp.zeros((TOK, FPAD), BF16)
     hb[:, 0:FFW] = hidden.astype(BF16)
     hb_copy = push(hb.at[:, 0:FPAD], hb.at[:, FPAD : 2 * FPAD], pr_ss.at[3], pr_rs.at[3], partner)
     wd_copy.wait_recv()

time: 72.7 us -> 72.9 us (level)
  no operation moved by 1% of the time
where the time goes in v5:
time: 72.9 us; the launch traced here: 72.8 us
  Pallas kernels  72.2 us (99%)
    pallas_call x1, Pallas kernels, layer(): pl.pallas_call(kernel, out_shape=pltpu.VMEM((2, DM), BF16), in_specs=[pl....  72.2 us

profile of v5, /device:TPU:1, one launch (start us, length us, event | category | flops | bytes accessed | tf_op | source)
XLA Modules:
  0.0 72.8 jit_solution(14242161644973124518)
XLA Ops:
  0.0 72.2 %layer.1 = bf16[2,4096]{1,0:T(2,128)(2,1)S(1)} custom-call(bf16[128,128]{1,0:T(8,128)(2,1)} %q_hbm.1, bf16[128,128]{1,0:T(8,128)(2,1)} %k_hbm.1, bf16[128,128]{1,0:T(8,128)(2,1)} %v_hbm.1, f32[1,128]{1,0:T(1,128)} %bitcast.16, bf16[1,128]{1,0:T(2,128)(2,1)} %bitcast.17, bf16[128,4096]{1,0:T(8,128)(2,1)} %wo_hbm.1, bf16[4,4096]{1,0:T(4,128)(2,1)} %bitcast.14, ...), custom_call_target="tpu_custom_call" | custom-call | tf_op jit(solution)/shard_map/layer/pallas_call | solution.py:453
  72.2 0.6 copy.13
